TPU v7x, 32 devices: a whole 2x2x4 slice. The times are simulated.
32 devices in a mesh: seq: 8 (over y, x, core), ch: 4 (over z).
Axes of the slice: x: 2, y: 2, z: 4, core: 2. Of those that a mesh axis runs over, the one named last changes fastest.
Arguments:
- streams: bfloat16 [3, 128, 8192], P(None, None, ('seq', 'ch')), may hold values from -6 to 6
- conv_taps: float32 [3, 128, 7], replicated, may hold values from -2.5 to 2.5
- long_filter: float32 [128, 8192], P('ch', 'seq'), may hold values from -0.06629126 to 0.06629126
- skip_gain: float32 [128], P('ch'), may hold values from -6 to 6
Outputs:
- mixer_output: bfloat16 [128, 8192], P(None, ('seq', 'ch'))
All inputs are finite; a program needn't handle non-finite values.
Results may differ from a plain program's by a relative error of at most 0.0064.
Values may be sent and summed in bfloat16 or wider, within the bound.
A program may use at most 64 MiB of HBM per device.

v0:
```python
import functools
import math

import jax
import jax.numpy as jnp
from jax import lax
from jax.experimental import pallas as pl
from jax.experimental.pallas import tpu as pltpu
from jax.sharding import PartitionSpec as P

BLOCK = 64
LANES = 128
GROUP = 4
SPAN = 8


highest = lax.Precision.HIGHEST
two_pi = 2.0 * math.pi


def from_behind(value, axis, steps):
    count = lax.axis_size(axis)
    initial, last = (max(0, -steps), min(count, count - steps))
    return lax.ppermute(value, axis, [(source, source + steps) for source in range(initial, last)])


def tables(row_count, col_count, period):
    grid = lax.broadcasted_iota(jnp.int32, (row_count, col_count), 0) * lax.broadcasted_iota(
        jnp.int32, (row_count, col_count), 1
    )
    angle = (grid % period).astype(jnp.float32) * (two_pi / period)
    return (jnp.cos(angle), jnp.sin(angle))


def short_filter(block_in, upstream, weights):
    tap_count = weights.shape[2]
    extended = jnp.concatenate([upstream, block_in], axis=2).astype(jnp.float32)
    length_here = block_in.shape[2]
    summed = jnp.zeros(block_in.shape, jnp.float32)
    for offset in range(tap_count):
        begin = tap_count - 1 - offset
        summed = (
            summed
            + weights[:, :, offset : offset + 1] * extended[:, :, begin : begin + length_here]
        )
    return summed.astype(jnp.bfloat16)


def rotate(real_part, imag_part, cosine, sine):
    return (real_part * cosine + imag_part * sine, imag_part * cosine - real_part * sine)


def dft_apply(real_part, imag_part, form, cosine, sine):
    first = jnp.einsum(form, real_part, cosine, precision=highest) + jnp.einsum(
        form, imag_part, sine, precision=highest
    )
    second = jnp.einsum(form, imag_part, cosine, precision=highest) - jnp.einsum(
        form, real_part, sine, precision=highest
    )
    return (first, second)


def section_one(moved, cos_seq, sin_seq, total_items, columns_each):
    family = moved.shape[0]
    real_part = jnp.einsum("fcst,sk->fckt", moved, cos_seq, precision=highest)
    imag_part = -jnp.einsum("fcst,sk->fckt", moved, sin_seq, precision=highest)
    return jnp.stack([real_part, imag_part]).reshape(2, family, total_items, columns_each)


def local(streams, conv_taps, long_filter, skip_gain):
    seq_count = lax.axis_size("seq")
    seq_pos = lax.axis_index("seq")
    group_pos = lax.axis_index("ch")
    channels = long_filter.shape[0]
    tokens_here = long_filter.shape[1]
    tap_count = conv_taps.shape[2]
    length = tokens_here * seq_count
    padded_len = 2 * length
    columns_each = tokens_here // seq_count
    doubled = 2 * seq_count
    item_count = channels * doubled // seq_count
    total_items = channels * doubled
    inner_len = tokens_here // BLOCK
    cos_seq, sin_seq = tables(seq_count, doubled, doubled)
    regrouped = lax.all_to_all(streams, "ch", split_axis=1, concat_axis=2, tiled=True)
    upstream = from_behind(regrouped[:, :, regrouped.shape[2] - (tap_count - 1) :], "seq", 1)
    own_taps = lax.dynamic_slice_in_dim(conv_taps, group_pos * channels, channels, 1)
    shorts = short_filter(regrouped, upstream, own_taps)
    queries = shorts[0].astype(jnp.float32)
    product = shorts[1].astype(jnp.float32) * shorts[2].astype(jnp.float32)
    both_moved = lax.all_to_all(
        jnp.stack([product, long_filter]).reshape(2, channels, 1, tokens_here),
        "seq",
        split_axis=3,
        concat_axis=2,
        tiled=True,
    )
    spectra_rows = lax.all_to_all(
        section_one(both_moved, cos_seq, sin_seq, total_items, columns_each),
        "seq",
        split_axis=2,
        concat_axis=3,
        tiled=True,
    )
    z_real = spectra_rows[0]
    z_imag = spectra_rows[1]
    cos_outer, sin_outer = tables(BLOCK, BLOCK, BLOCK)
    cos_inner, sin_inner = tables(inner_len, inner_len, inner_len)
    cos_mid, sin_mid = tables(BLOCK, inner_len, tokens_here)
    global_item = seq_pos * item_count + lax.iota(jnp.int32, item_count)
    freq = global_item % doubled
    twiddle_grid = lax.iota(jnp.int32, tokens_here)[None, :] * freq[:, None] % padded_len
    twiddle_angle = twiddle_grid.astype(jnp.float32) * (two_pi / padded_len)
    cos_twiddle = jnp.cos(twiddle_angle)
    sin_twiddle = jnp.sin(twiddle_angle)
    z_real, z_imag = rotate(z_real, z_imag, cos_twiddle, sin_twiddle)
    family = z_real.shape[0]
    z_real = z_real.reshape(family, item_count, BLOCK, inner_len)
    z_imag = z_imag.reshape(family, item_count, BLOCK, inner_len)
    z_real, z_imag = dft_apply(z_real, z_imag, "fiab,ae->fieb", cos_outer, sin_outer)
    z_real, z_imag = rotate(z_real, z_imag, cos_mid, sin_mid)
    z_real, z_imag = dft_apply(z_real, z_imag, "fieb,bg->fieg", cos_inner, sin_inner)
    prod_real = z_real[0] * z_real[1] - z_imag[0] * z_imag[1]
    prod_imag = z_real[0] * z_imag[1] + z_imag[0] * z_real[1]
    prod_real, prod_imag = dft_apply(prod_real, prod_imag, "ieg,gb->ieb", cos_inner, -sin_inner)
    prod_real, prod_imag = rotate(prod_real, prod_imag, cos_mid, -sin_mid)
    prod_real, prod_imag = dft_apply(prod_real, prod_imag, "ieb,ea->iab", cos_outer, -sin_outer)
    prod_real = prod_real.reshape(item_count, tokens_here)
    prod_imag = prod_imag.reshape(item_count, tokens_here)
    prod_real, prod_imag = rotate(prod_real, prod_imag, cos_twiddle, -sin_twiddle)
    returned = lax.all_to_all(
        jnp.stack([prod_real, prod_imag]), "seq", split_axis=2, concat_axis=1, tiled=True
    )
    returned = returned.reshape(2, channels, doubled, columns_each)
    partial_out = jnp.einsum("ckt,sk->cst", returned[0], cos_seq, precision=highest) - jnp.einsum(
        "ckt,sk->cst", returned[1], sin_seq, precision=highest
    )
    partial_out = partial_out * (1.0 / padded_len)
    longconv = lax.all_to_all(partial_out, "seq", split_axis=1, concat_axis=2, tiled=True).reshape(
        channels, tokens_here
    )
    gated = (queries * (longconv + skip_gain[:, None] * product)).astype(jnp.bfloat16)
    return lax.all_to_all(gated, "ch", split_axis=1, concat_axis=0, tiled=True)

MESH = pl.DeviceIdType.MESH


def owner_kernel(
    seq_count,
    ch_count,
    tap_count,
    streams,
    filt,
    aux,
    out,
    send_x,
    send_f,
    got_x,
    got_f,
    rows,
    done,
    send_o,
    got_o,
    wheel,
    x_send,
    x_recv,
    f_send,
    f_recv,
    o_send,
    o_recv,
):
    count = seq_count * ch_count
    seq_pos, ch_pos = lax.axis_index("seq"), lax.axis_index("ch")
    me = seq_pos * ch_count + ch_pos
    mine = ch_pos * seq_count + seq_pos
    width = streams.shape[2]
    span_f = filt.shape[1]
    blocks = width * count // LANES
    halves = width // LANES
    base = 8 * blocks

    def peer(step):
        other = lax.rem(me + step, count)
        return other, other // ch_count, lax.rem(other, ch_count)

    barrier = pltpu.get_barrier_semaphore()

    @pl.loop(1, count)
    def _(step):
        _, s, c = peer(step)
        pl.semaphore_signal(barrier, inc=1, device_id=(s, c), device_id_type=MESH)

    for s in range(seq_count):
        send_f[s] = filt[GROUP * s : GROUP * (s + 1), :]

    @pl.loop(0, streams.shape[1] // 16)
    def _(m):
        at = pl.ds(pl.multiple_of(16 * m, 16), 16)
        q, k, v = [streams[i, at, :].astype(jnp.float32) for i in range(3)]
        for e in range(4):
            part = slice(4 * e, 4 * e + 4)
            send_x[4 * m + e] = jnp.concatenate([q[part], k[part], v[part], v[part]], axis=0).astype(jnp.bfloat16)

    pl.semaphore_wait(barrier, count - 1)

    def filter_copy(s_to, s_from):
        at = pl.ds(pl.multiple_of(s_from * span_f, LANES), span_f)
        return pltpu.make_async_remote_copy(
            src_ref=send_f.at[s_to],
            dst_ref=got_f.at[:, at],
            send_sem=f_send.at[s_to],
            recv_sem=f_recv.at[s_from],
            device_id=(s_to, ch_pos),
            device_id_type=MESH,
        )

    def stream_copy(other, s, c, source):
        at = pl.ds(pl.multiple_of(LANES + source * width, LANES), width)
        block = c * seq_count + s
        return pltpu.make_async_remote_copy(
            src_ref=send_x.at[block],
            dst_ref=got_x.at[:, at],
            send_sem=x_send.at[other],
            recv_sem=x_recv.at[source],
            device_id=(s, c),
            device_id_type=MESH,
        )

    def out_copy(other, s, c, source):
        return pltpu.make_async_remote_copy(
            src_ref=send_o.at[other],
            dst_ref=got_o.at[source],
            send_sem=o_send.at[other],
            recv_sem=o_recv.at[source],
            device_id=(s, c),
            device_id_type=MESH,
        )

    @pl.loop(1, seq_count)
    def _(step):
        filter_copy(lax.rem(seq_pos + step, seq_count), seq_pos).start()

    @pl.loop(1, count)
    def _(step):
        other, s, c = peer(step)
        stream_copy(other, s, c, me).start()

    got_f[:, pl.ds(pl.multiple_of(seq_pos * span_f, LANES), span_f)] = send_f[seq_pos]
    got_x[:, pl.ds(pl.multiple_of(LANES + me * width, LANES), width)] = send_x[mine]
    got_x[:, 0:LANES] = jnp.zeros((16, LANES), jnp.bfloat16)
    rows[0:base, :] = jnp.zeros((base, LANES), jnp.float32)

    @pl.loop(1, seq_count)
    def _(step):
        filter_copy(lax.rem(seq_pos + step, seq_count), lax.rem(seq_pos + step, seq_count)).wait_recv()

    @pl.loop(1, count)
    def _(step):
        other, s, c = peer(step)
        stream_copy(other, s, c, other).wait_recv()

    chunk = 4 * LANES
    taps = [jnp.concatenate([aux[j]] * 4, axis=1) for j in range(tap_count)]

    @pl.loop(0, blocks // 4)
    def _(i):
        ext = got_x[:, pl.ds(pl.multiple_of(i * chunk, LANES), chunk + LANES)].astype(jnp.float32)
        total = taps[0] * ext[:, LANES:]
        for j in range(1, tap_count):
            total = total + taps[j] * pltpu.roll(ext, j, 1)[:, LANES:]
        shorts = total.astype(jnp.bfloat16).astype(jnp.float32)
        product = shorts[4:8] * shorts[8:12]
        both = jnp.concatenate([product, shorts[0:4]], axis=0)
        for u in range(4):
            rows[pl.ds(pl.multiple_of(base + 8 * (4 * i + u), 8), 8), :] = both[:, LANES * u : LANES * (u + 1)]

    row_at = lax.broadcasted_iota(jnp.int32, (LANES, LANES), 0)
    lane_at = lax.broadcasted_iota(jnp.int32, (LANES, LANES), 1)
    upper = lane_at >= row_at

    for c in range(GROUP):
        wheel[...] = jnp.zeros_like(wheel)

        def body(big, total):
            last = wheel[...]
            lags, shifted = [], []
            for u in range(SPAN):
                d = big * SPAN + u
                h = got_f[c : c + 1, pl.ds(pl.multiple_of(d * LANES, LANES), LANES)]
                turn = pltpu.roll(jnp.broadcast_to(h, (LANES, LANES)), 0, 1, stride=1, stride_axis=0)
                lags.append(jnp.where(upper, turn, last).astype(jnp.bfloat16))
                shifted.append(rows[pl.ds(base + c - 8 * d, blocks, stride=8), :].astype(jnp.bfloat16))
                last = turn
            wheel[...] = last
            return total + jnp.dot(
                jnp.concatenate(shifted, axis=1),
                jnp.concatenate(lags, axis=0),
                preferred_element_type=jnp.float32,
            )

        conv = lax.fori_loop(0, blocks // SPAN, body, jnp.zeros((blocks, LANES), jnp.float32))
        product = rows[pl.ds(base + c, blocks, stride=8), :]
        q = rows[pl.ds(base + GROUP + c, blocks, stride=8), :]
        gain = aux[tap_count, c : c + 1, :]
        done[pl.ds(c, blocks, stride=GROUP), :] = q * (conv + gain * product)

    @pl.loop(0, count)
    def _(t):
        send_o[t] = done[pl.ds(pl.multiple_of(8 * t, 8), 8), :].astype(send_o.dtype)

    @pl.loop(1, count)
    def _(step):
        other, s, c = peer(step)
        out_copy(other, s, c, mine).start()

    got_o[mine] = send_o[me]

    @pl.loop(1, count)
    def _(step):
        other, s, c = peer(step)
        out_copy(other, s, c, c * seq_count + s).wait_recv()

    @pl.loop(0, count // 4)
    def _(m):
        parts = [got_o[4 * m + e].astype(jnp.float32) for e in range(4)]
        at = pl.ds(pl.multiple_of(16 * m, 16), 16)
        for half in range(2):
            piece = jnp.concatenate([p[4 * half : 4 * half + 4] for p in parts], axis=0)
            out[at, LANES * half : LANES * (half + 1)] = piece.astype(jnp.bfloat16)

    @pl.loop(1, seq_count)
    def _(step):
        filter_copy(lax.rem(seq_pos + step, seq_count), seq_pos).wait_send()

    @pl.loop(1, count)
    def _(step):
        other, s, c = peer(step)
        stream_copy(other, s, c, me).wait_send()
        out_copy(other, s, c, mine).wait_send()


def owner_local(streams, conv_taps, long_filter, skip_gain):
    seq_count, ch_count = lax.axis_size("seq"), lax.axis_size("ch")
    seq_pos, ch_pos = lax.axis_index("seq"), lax.axis_index("ch")
    count = seq_count * ch_count
    channels, width = streams.shape[1:]
    tap_count = conv_taps.shape[2]
    length = width * count
    mine = ch_pos * seq_count + seq_pos
    own_taps = lax.dynamic_slice_in_dim(conv_taps, mine * GROUP, GROUP, 1).reshape(3 * GROUP, tap_count)
    own_taps = jnp.pad(own_taps.T, ((0, 0), (0, GROUP)))
    own_gain = jnp.pad(lax.dynamic_slice_in_dim(skip_gain, seq_pos * GROUP, GROUP, 0), (0, 3 * GROUP))
    aux = jnp.concatenate([own_taps, own_gain[None]], axis=0)
    aux = jnp.broadcast_to(aux[:, :, None], aux.shape + (LANES,))
    blocks = length // LANES
    dma = pltpu.SemaphoreType.DMA
    return pl.pallas_call(
        functools.partial(owner_kernel, seq_count, ch_count, tap_count),
        out_shape=jax.ShapeDtypeStruct((channels, width), jnp.bfloat16),
        in_specs=[pl.BlockSpec(memory_space=pltpu.VMEM)] * 3,
        out_specs=pl.BlockSpec(memory_space=pltpu.VMEM),
        scratch_shapes=[
            pltpu.VMEM((count, 16, width), jnp.bfloat16),
            pltpu.VMEM((seq_count, GROUP, long_filter.shape[1]), jnp.float32),
            pltpu.VMEM((16, LANES + length), jnp.bfloat16),
            pltpu.VMEM((GROUP, length), jnp.float32),
            pltpu.VMEM((16 * blocks, LANES), jnp.float32),
            pltpu.VMEM((GROUP * blocks, LANES), jnp.float32),
            pltpu.VMEM((count, 8, LANES), jnp.bfloat16),
            pltpu.VMEM((count, 8, LANES), jnp.bfloat16),
            pltpu.VMEM((LANES, LANES), jnp.float32),
            dma((count,)),
            dma((count,)),
            dma((seq_count,)),
            dma((seq_count,)),
            dma((count,)),
            dma((count,)),
        ],
        compiler_params=pltpu.CompilerParams(
            collective_id=0, has_side_effects=True, vmem_limit_bytes=32 * 1024 * 1024
        ),
    )(streams, long_filter, aux)


def pick(streams, conv_taps, long_filter, skip_gain):
    count = lax.axis_size("seq") * lax.axis_size("ch")
    fits = streams.shape[1] == GROUP * count and streams.shape[2] == 2 * LANES and count % 4 == 0
    return (owner_local if fits else local)(streams, conv_taps, long_filter, skip_gain)


def solution(mesh):
    return jax.shard_map(
        pick,
        mesh=mesh,
        in_specs=(P(None, None, ("seq", "ch")), P(), P("ch", "seq"), P("ch")),
        out_specs=P(None, ("seq", "ch")),
        check_vma=False,
    )
```

profile of v0, /device:TPU:0, one launch (start us, length us, event | category | flops | bytes accessed | tf_op | source)
XLA Modules:
  0.0 36.7 jit_solution(4961705352273603082)
XLA Ops:
  0.0 0.0 copy-start
  0.0 0.0 copy-start.1
  0.0 0.8 %dynamic_slice.7 = f32[4]{0:T(128)S(1)} dynamic-slice(f32[32]{0:T(128)} %param.7, s32[]{:T(128)S(6)} %select_n.7), dynamic_slice_sizes={4} | dynamic-slice | bytes 36 | tf_op jit(solution)/shard_map/dynamic_slice | solution.py:352
  0.8 0.1 copy.9
  0.9 0.0 copy-done
  0.9 0.1 constant_dynamic-slice_fusion
  0.9 0.1 copy.8
  1.1 0.1 select_maximum_fusion
  1.1 0.1 copy.10
  1.2 0.1 broadcast_in_dim.10.aux
  1.3 0.0 copy-done.1
  1.3 0.0 copy-start.2
  1.3 0.9 %copy-done.2 = f32[32,1024]{1,0:T(8,128)S(1)} copy-done((f32[32,1024]{1,0:T(8,128)S(1)}, f32[32,1024]{1,0:T(8,128)}, u32[]{:S(2)}) %copy-start.2) | copy-done | bytes 131096
  2.2 33.9 %shard_map.46 = bf16[128,256]{1,0:T(8,128)(2,1)S(1)} custom-call(bf16[3,128,256]{2,1,0:T(8,128)(2,1)S(1)} %copy-done.1, f32[32,1024]{1,0:T(8,128)S(1)} %copy-done.2, f32[8,16,128]{2,1,0:T(8,128)S(1)} %broadcast_in_dim.10.aux), custom_call_target="tpu_custom_call" | custom-call | tf_op jit(solution)/shard_map/pallas_call | solution.py:357
  36.1 0.6 %copy.12 = bf16[128,256]{1,0:T(8,128)(2,1)} copy(bf16[128,256]{1,0:T(8,128)(2,1)S(1)} %shard_map.46) | data formatting | bytes 131072
  (2 shorter events, 0.0 us)
Async XLA Ops:
  0.0 0.9 %copy-start = (f32[3,128,7]{1,2,0:T(8,128)S(1)}, f32[3,128,7]{1,2,0:T(8,128)}, u32[]{:S(2)}) copy-start(f32[3,128,7]{1,2,0:T(8,128)} %param.5) | copy-start | bytes 32260
  0.0 1.3 %copy-start.1 = (bf16[3,128,256]{2,1,0:T(8,128)(2,1)S(1)}, bf16[3,128,256]{2,1,0:T(8,128)(2,1)}, u32[]{:S(2)}) copy-start(bf16[3,128,256]{2,1,0:T(8,128)(2,1)} %streams.1) | copy-start | bytes 589828
  1.3 0.9 %copy-start.2 = (f32[32,1024]{1,0:T(8,128)S(1)}, f32[32,1024]{1,0:T(8,128)}, u32[]{:S(2)}) copy-start(f32[32,1024]{1,0:T(8,128)} %filt.1) | copy-start | bytes 393220
where the time goes:
time: 36.9 us; the launch traced here: 36.7 us
  Pallas kernels  33.9 us (92%)
  local copies, waits for them, and re-layouts  2.74 us (7%)
    pallas_call x1, Pallas kernels, owner_local(): pl.pallas_call(functools.partial(owner_kernel, seq_count, ch_count, tap_c...  33.9 us
    unnamed x7, local copies, waits for them, and re-layouts  1.55 us
    dynamic_slice x1, local copies, waits for them, and re-layouts, owner_local(): lax.dynamic_slice_in_dim(skip_gain, seq_pos * GROUP, GROUP, 0)  0.77 us

commit v1 on v0

--- a/solution.py
+++ b/solution.py
@@ -148,20 +148,25 @@
 def owner_kernel(
     seq_count,
     ch_count,
-    tap_count,
+    streams_in,
+    filt_in,
+    taps_in,
+    gains_in,
+    out,
     streams,
     filt,
-    aux,
-    out,
     send_x,
     send_f,
     got_x,
     got_f,
+    tap_rows,
     rows,
+    lags,
     done,
+    part,
     send_o,
     got_o,
-    wheel,
+    load_sem,
     x_send,
     x_recv,
     f_send,
@@ -175,9 +180,11 @@
     mine = ch_pos * seq_count + seq_pos
     width = streams.shape[2]
     span_f = filt.shape[1]
+    tap_count = taps_in.shape[1]
     blocks = width * count // LANES
-    halves = width // LANES
+    half = blocks // 2
     base = 8 * blocks
+    f32, bf16 = jnp.float32, jnp.bfloat16
 
     def peer(step):
         other = lax.rem(me + step, count)
@@ -190,21 +197,37 @@
         _, s, c = peer(step)
         pl.semaphore_signal(barrier, inc=1, device_id=(s, c), device_id_type=MESH)
 
+    load_f = pltpu.make_async_copy(filt_in, filt, load_sem.at[0])
+    load_x = pltpu.make_async_copy(streams_in, streams, load_sem.at[1])
+    load_f.start()
+    load_x.start()
+    lane = lax.broadcasted_iota(jnp.int32, (tap_count, LANES), 1)
+    for c in range(GROUP):
+        for i in range(3):
+            column = jnp.sum(jnp.where(lane == GROUP * mine + c, taps_in[i], 0.0), axis=1, keepdims=True)
+            tap_rows[pl.ds(32 * i + c, tap_count, stride=GROUP), :] = jnp.broadcast_to(column, (tap_count, LANES))
+    rows[0:base, :] = jnp.zeros((base, LANES), f32)
+    for i in range(3):
+        got_x[i, :, 0:LANES] = jnp.zeros((GROUP, LANES), bf16)
+    got_f[:, 0:LANES] = jnp.zeros((GROUP, LANES), bf16)
+
+    load_f.wait()
     for s in range(seq_count):
-        send_f[s] = filt[GROUP * s : GROUP * (s + 1), :]
+        send_f[s] = filt[GROUP * s : GROUP * (s + 1), :].astype(bf16)
+    load_x.wait()
 
     @pl.loop(0, streams.shape[1] // 16)
     def _(m):
         at = pl.ds(pl.multiple_of(16 * m, 16), 16)
-        q, k, v = [streams[i, at, :].astype(jnp.float32) for i in range(3)]
-        for e in range(4):
-            part = slice(4 * e, 4 * e + 4)
-            send_x[4 * m + e] = jnp.concatenate([q[part], k[part], v[part], v[part]], axis=0).astype(jnp.bfloat16)
+        for i in range(3):
+            values = streams[i, at, :].astype(f32)
+            for e in range(4):
+                send_x[4 * m + e, i] = values[4 * e : 4 * e + 4].astype(bf16)
 
     pl.semaphore_wait(barrier, count - 1)
 
     def filter_copy(s_to, s_from):
-        at = pl.ds(pl.multiple_of(s_from * span_f, LANES), span_f)
+        at = pl.ds(pl.multiple_of(LANES + s_from * span_f, LANES), span_f)
         return pltpu.make_async_remote_copy(
             src_ref=send_f.at[s_to],
             dst_ref=got_f.at[:, at],
@@ -219,20 +242,20 @@
         block = c * seq_count + s
         return pltpu.make_async_remote_copy(
             src_ref=send_x.at[block],
-            dst_ref=got_x.at[:, at],
+            dst_ref=got_x.at[:, :, at],
             send_sem=x_send.at[other],
             recv_sem=x_recv.at[source],
             device_id=(s, c),
             device_id_type=MESH,
         )
 
-    def out_copy(other, s, c, source):
+    def out_copy(other, source):
         return pltpu.make_async_remote_copy(
             src_ref=send_o.at[other],
             dst_ref=got_o.at[source],
             send_sem=o_send.at[other],
             recv_sem=o_recv.at[source],
-            device_id=(s, c),
+            device_id=(other // ch_count, lax.rem(other, ch_count)),
             device_id_type=MESH,
         )
 
@@ -245,130 +268,155 @@
         other, s, c = peer(step)
         stream_copy(other, s, c, me).start()
 
-    got_f[:, pl.ds(pl.multiple_of(seq_pos * span_f, LANES), span_f)] = send_f[seq_pos]
-    got_x[:, pl.ds(pl.multiple_of(LANES + me * width, LANES), width)] = send_x[mine]
-    got_x[:, 0:LANES] = jnp.zeros((16, LANES), jnp.bfloat16)
-    rows[0:base, :] = jnp.zeros((base, LANES), jnp.float32)
+    got_f[:, pl.ds(pl.multiple_of(LANES + seq_pos * span_f, LANES), span_f)] = send_f[seq_pos]
+    for i in range(3):
+        got_x[i, :, pl.ds(pl.multiple_of(LANES + me * width, LANES), width)] = send_x[mine, i]
 
     @pl.loop(1, seq_count)
     def _(step):
-        filter_copy(lax.rem(seq_pos + step, seq_count), lax.rem(seq_pos + step, seq_count)).wait_recv()
-
-    @pl.loop(1, count)
-    def _(step):
-        other, s, c = peer(step)
-        stream_copy(other, s, c, other).wait_recv()
-
-    chunk = 4 * LANES
-    taps = [jnp.concatenate([aux[j]] * 4, axis=1) for j in range(tap_count)]
-
-    @pl.loop(0, blocks // 4)
-    def _(i):
-        ext = got_x[:, pl.ds(pl.multiple_of(i * chunk, LANES), chunk + LANES)].astype(jnp.float32)
-        total = taps[0] * ext[:, LANES:]
-        for j in range(1, tap_count):
-            total = total + taps[j] * pltpu.roll(ext, j, 1)[:, LANES:]
-        shorts = total.astype(jnp.bfloat16).astype(jnp.float32)
-        product = shorts[4:8] * shorts[8:12]
-        both = jnp.concatenate([product, shorts[0:4]], axis=0)
-        for u in range(4):
-            rows[pl.ds(pl.multiple_of(base + 8 * (4 * i + u), 8), 8), :] = both[:, LANES * u : LANES * (u + 1)]
+        source = lax.rem(seq_pos + step, seq_count)
+        filter_copy(source, source).wait_recv()
 
     row_at = lax.broadcasted_iota(jnp.int32, (LANES, LANES), 0)
     lane_at = lax.broadcasted_iota(jnp.int32, (LANES, LANES), 1)
     upper = lane_at >= row_at
 
+    @pl.loop(0, blocks // SPAN)
+    def _(big):
+        wide = SPAN * LANES
+        window = got_f[:, pl.ds(pl.multiple_of(big * wide, LANES), wide + LANES)].astype(f32)
+        for c in range(GROUP):
+            last = None
+            for u in range(SPAN + 1):
+                h = jnp.broadcast_to(window[c : c + 1, LANES * u : LANES * (u + 1)], (LANES, LANES))
+                turn = pltpu.roll(h, 0, 1, stride=1, stride_axis=0)
+                if u > 0:
+                    at = pl.ds(pl.multiple_of((big * SPAN + u - 1) * LANES, LANES), LANES)
+                    lags[c, at, :] = jnp.where(upper, turn, last).astype(bf16)
+                last = turn
+
+    chunk = 4 * LANES
+    taps = []
+    for j in range(tap_count):
+        r = [tap_rows[32 * i + GROUP * j : 32 * i + GROUP * j + GROUP, :] for i in range(3)]
+        qk = jnp.concatenate(r[:2], axis=0)
+        taps.append([jnp.concatenate([t] * 4, axis=1) for t in (qk, r[2])])
+
+    @pl.loop(0, blocks // 4)
+    def _(n):
+        for e in range(2):
+            source = 2 * n + e
+
+            @pl.when(source != me)
+            def _():
+                stream_copy(source, source // ch_count, lax.rem(source, ch_count), source).wait_recv()
+
+        at = pl.ds(pl.multiple_of(n * chunk, LANES), chunk + LANES)
+        q, k, v = [got_x[i, :, at].astype(f32) for i in range(3)]
+        shorts = []
+        for which, ext in enumerate((jnp.concatenate([q, k], axis=0), v)):
+            total = taps[0][which] * ext[:, LANES:]
+            for j in range(1, tap_count):
+                total = total + taps[j][which] * pltpu.roll(ext, j, 1)[:, LANES:]
+            shorts.append(total.astype(bf16).astype(f32))
+        product = shorts[0][GROUP:] * shorts[1]
+        both = jnp.concatenate([product, shorts[0][:GROUP]], axis=0)
+        for u in range(4):
+            rows[pl.ds(pl.multiple_of(base + 8 * (4 * n + u), 8), 8), :] = both[:, LANES * u : LANES * (u + 1)]
+
+    gain_lane = lax.broadcasted_iota(jnp.int32, gains_in.shape, 1)
+
+    def partial_conv(c, first, many, d_from):
+        at = [pl.ds(base + c + 8 * (first - d), many, stride=8) for d in range(d_from, d_from + half)]
+        shifted = jnp.concatenate([rows[a, :].astype(bf16) for a in at], axis=1)
+        return jnp.dot(shifted, lags[c, LANES * d_from : LANES * (d_from + half), :], preferred_element_type=f32)
+
+    def finish(c, first, conv):
+        product = rows[pl.ds(base + 8 * first + c, half, stride=8), :]
+        q = rows[pl.ds(base + 8 * first + GROUP + c, half, stride=8), :]
+        gain = jnp.sum(jnp.where(gain_lane == GROUP * seq_pos + c, gains_in[...], 0.0), axis=1, keepdims=True)
+        done[pl.ds(GROUP * first + c, half, stride=GROUP), :] = q * (conv + gain * product)
+
+    def send_half(first):
+        for t in range(first, first + count // 2):
+            send_o[t] = done[8 * t : 8 * t + 8, :].astype(bf16)
+
+        @pl.loop(0, count // 2)
+        def _(step):
+            other = first + lax.rem(me + step, count // 2)
+
+            @pl.when(other != me)
+            def _():
+                out_copy(other, mine).start()
+
     for c in range(GROUP):
-        wheel[...] = jnp.zeros_like(wheel)
-
-        def body(big, total):
-            last = wheel[...]
-            lags, shifted = [], []
-            for u in range(SPAN):
-                d = big * SPAN + u
-                h = got_f[c : c + 1, pl.ds(pl.multiple_of(d * LANES, LANES), LANES)]
-                turn = pltpu.roll(jnp.broadcast_to(h, (LANES, LANES)), 0, 1, stride=1, stride_axis=0)
-                lags.append(jnp.where(upper, turn, last).astype(jnp.bfloat16))
-                shifted.append(rows[pl.ds(base + c - 8 * d, blocks, stride=8), :].astype(jnp.bfloat16))
-                last = turn
-            wheel[...] = last
-            return total + jnp.dot(
-                jnp.concatenate(shifted, axis=1),
-                jnp.concatenate(lags, axis=0),
-                preferred_element_type=jnp.float32,
-            )
-
-        conv = lax.fori_loop(0, blocks // SPAN, body, jnp.zeros((blocks, LANES), jnp.float32))
-        product = rows[pl.ds(base + c, blocks, stride=8), :]
-        q = rows[pl.ds(base + GROUP + c, blocks, stride=8), :]
-        gain = aux[tap_count, c : c + 1, :]
-        done[pl.ds(c, blocks, stride=GROUP), :] = q * (conv + gain * product)
-
-    @pl.loop(0, count)
-    def _(t):
-        send_o[t] = done[pl.ds(pl.multiple_of(8 * t, 8), 8), :].astype(send_o.dtype)
+        conv = partial_conv(c, 0, blocks, 0)
+        finish(c, 0, conv[:half])
+        part[c] = conv[half:]
+    send_half(0)
+    for c in range(GROUP):
+        finish(c, half, part[c] + partial_conv(c, half, half, half))
+    send_half(count // 2)
+
+    got_o[mine] = send_o[me]
+
+    @pl.loop(1, seq_count)
+    def _(step):
+        filter_copy(lax.rem(seq_pos + step, seq_count), seq_pos).wait_send()
 
     @pl.loop(1, count)
     def _(step):
         other, s, c = peer(step)
-        out_copy(other, s, c, mine).start()
-
-    got_o[mine] = send_o[me]
+        stream_copy(other, s, c, me).wait_send()
 
     @pl.loop(1, count)
     def _(step):
         other, s, c = peer(step)
-        out_copy(other, s, c, c * seq_count + s).wait_recv()
+        out_copy(other, c * seq_count + s).wait_recv()
 
     @pl.loop(0, count // 4)
     def _(m):
-        parts = [got_o[4 * m + e].astype(jnp.float32) for e in range(4)]
+        parts = [got_o[4 * m + e].astype(f32) for e in range(4)]
         at = pl.ds(pl.multiple_of(16 * m, 16), 16)
-        for half in range(2):
-            piece = jnp.concatenate([p[4 * half : 4 * half + 4] for p in parts], axis=0)
-            out[at, LANES * half : LANES * (half + 1)] = piece.astype(jnp.bfloat16)
-
-    @pl.loop(1, seq_count)
-    def _(step):
-        filter_copy(lax.rem(seq_pos + step, seq_count), seq_pos).wait_send()
+        for side in range(2):
+            piece = jnp.concatenate([p[4 * side : 4 * side + 4] for p in parts], axis=0)
+            out[at, LANES * side : LANES * (side + 1)] = piece.astype(bf16)
 
     @pl.loop(1, count)
     def _(step):
-        other, s, c = peer(step)
-        stream_copy(other, s, c, me).wait_send()
-        out_copy(other, s, c, mine).wait_send()
+        out_copy(lax.rem(me + step, count), mine).wait_send()
 
 
 def owner_local(streams, conv_taps, long_filter, skip_gain):
     seq_count, ch_count = lax.axis_size("seq"), lax.axis_size("ch")
-    seq_pos, ch_pos = lax.axis_index("seq"), lax.axis_index("ch")
     count = seq_count * ch_count
     channels, width = streams.shape[1:]
-    tap_count = conv_taps.shape[2]
     length = width * count
-    mine = ch_pos * seq_count + seq_pos
-    own_taps = lax.dynamic_slice_in_dim(conv_taps, mine * GROUP, GROUP, 1).reshape(3 * GROUP, tap_count)
-    own_taps = jnp.pad(own_taps.T, ((0, 0), (0, GROUP)))
-    own_gain = jnp.pad(lax.dynamic_slice_in_dim(skip_gain, seq_pos * GROUP, GROUP, 0), (0, 3 * GROUP))
-    aux = jnp.concatenate([own_taps, own_gain[None]], axis=0)
-    aux = jnp.broadcast_to(aux[:, :, None], aux.shape + (LANES,))
     blocks = length // LANES
     dma = pltpu.SemaphoreType.DMA
+    f32, bf16 = jnp.float32, jnp.bfloat16
+    anywhere = pl.BlockSpec(memory_space=pl.ANY)
+    inside = pl.BlockSpec(memory_space=pltpu.VMEM)
     return pl.pallas_call(
-        functools.partial(owner_kernel, seq_count, ch_count, tap_count),
-        out_shape=jax.ShapeDtypeStruct((channels, width), jnp.bfloat16),
-        in_specs=[pl.BlockSpec(memory_space=pltpu.VMEM)] * 3,
-        out_specs=pl.BlockSpec(memory_space=pltpu.VMEM),
+        functools.partial(owner_kernel, seq_count, ch_count),
+        out_shape=jax.ShapeDtypeStruct((channels, width), bf16),
+        in_specs=[anywhere, anywhere, inside, inside],
+        out_specs=inside,
         scratch_shapes=[
-            pltpu.VMEM((count, 16, width), jnp.bfloat16),
-            pltpu.VMEM((seq_count, GROUP, long_filter.shape[1]), jnp.float32),
-            pltpu.VMEM((16, LANES + length), jnp.bfloat16),
-            pltpu.VMEM((GROUP, length), jnp.float32),
-            pltpu.VMEM((16 * blocks, LANES), jnp.float32),
-            pltpu.VMEM((GROUP * blocks, LANES), jnp.float32),
-            pltpu.VMEM((count, 8, LANES), jnp.bfloat16),
-            pltpu.VMEM((count, 8, LANES), jnp.bfloat16),
-            pltpu.VMEM((LANES, LANES), jnp.float32),
+            pltpu.VMEM(streams.shape, bf16),
+            pltpu.VMEM(long_filter.shape, f32),
+            pltpu.VMEM((count, 3, GROUP, width), bf16),
+            pltpu.VMEM((seq_count, GROUP, long_filter.shape[1]), bf16),
+            pltpu.VMEM((3, GROUP, LANES + length), bf16),
+            pltpu.VMEM((GROUP, LANES + length), bf16),
+            pltpu.VMEM((96, LANES), f32),
+            pltpu.VMEM((16 * blocks, LANES), f32),
+            pltpu.VMEM((GROUP, length, LANES), bf16),
+            pltpu.VMEM((GROUP * blocks, LANES), f32),
+            pltpu.VMEM((GROUP, blocks // 2, LANES), f32),
+            pltpu.VMEM((count, 8, LANES), bf16),
+            pltpu.VMEM((count, 8, LANES), bf16),
+            dma((2,)),
             dma((count,)),
             dma((count,)),
             dma((seq_count,)),
@@ -377,14 +425,16 @@
             dma((count,)),
         ],
         compiler_params=pltpu.CompilerParams(
-            collective_id=0, has_side_effects=True, vmem_limit_bytes=32 * 1024 * 1024
+            collective_id=0, has_side_effects=True, vmem_limit_bytes=48 * 1024 * 1024
         ),
-    )(streams, long_filter, aux)
+    )(streams, long_filter, jnp.swapaxes(conv_taps, 1, 2), skip_gain[None, :])
 
 
 def pick(streams, conv_taps, long_filter, skip_gain):
     count = lax.axis_size("seq") * lax.axis_size("ch")
-    fits = streams.shape[1] == GROUP * count and streams.shape[2] == 2 * LANES and count % 4 == 0
+    tap_fit = conv_taps.shape[2] <= 8
+    tokens_fit = streams.shape[2] == 2 * LANES and streams.shape[1] == LANES
+    fits = streams.shape[1] == GROUP * count and tokens_fit and tap_fit
     return (owner_local if fits else local)(streams, conv_taps, long_filter, skip_gain)
 
 

time: 36.9 us -> 26.9 us (0.73)
  Pallas kernels: 33.9 us -> 22.8 us
  local copies, waits for them, and re-layouts: 2.74 us -> 3.82 us
    pallas_call x1, Pallas kernels: 33.9 us -> 22.8 us  [owner_local(): pl.pallas_call(functools.partial(owner_kernel, seq_count, ch_count), out_...]
    unnamed x7 -> x9, local copies, waits for them, and re-layouts: 1.55 us -> 3.82 us
    dynamic_slice x3 -> x0, local copies, waits for them, and re-layouts: 0.95 us -> none  [the longest x1 0.77 us: owner_local(): lax.dynamic_slice_in_dim(skip_gain, seq_pos * GROUP, GROUP, 0)]
where the time goes in v1:
time: 26.9 us; the launch traced here: 26.7 us
  Pallas kernels  22.8 us (85%)
  local copies, waits for them, and re-layouts  3.82 us (14%)
    pallas_call x1, Pallas kernels, owner_local(): pl.pallas_call(functools.partial(owner_kernel, seq_count, ch_count), out_...  22.8 us
    unnamed x9, local copies, waits for them, and re-layouts  3.82 us

profile of v1, /device:TPU:0, one launch (start us, length us, event | category | flops | bytes accessed | tf_op | source)
XLA Modules:
  0.0 26.7 jit_solution(14917144688280728957)
XLA Ops:
  0.0 0.0 copy-start.3
  0.0 0.7 %copy-done.3 = f32[32]{0:T(128)S(1)} copy-done((f32[32]{0:T(128)S(1)}, f32[32]{0:T(128)}, u32[]{:S(2)}) %copy-start.3) | copy-done | bytes 152
  0.7 0.0 copy-start
  0.7 0.9 %copy-done = bf16[3,128,256]{2,1,0:T(8,128)(2,1)S(1)} copy-done((bf16[3,128,256]{2,1,0:T(8,128)(2,1)S(1)}, bf16[3,128,256]{2,1,0:T(8,128)(2,1)}, u32[]{:S(2)}) %copy-start) | copy-done | bytes 196632
  1.6 0.0 copy-start.1
  1.6 0.9 %copy-done.1 = f32[32,1024]{1,0:T(8,128)S(1)} copy-done((f32[32,1024]{1,0:T(8,128)S(1)}, f32[32,1024]{1,0:T(8,128)}, u32[]{:S(2)}) %copy-start.1) | copy-done | bytes 131096
  2.5 0.0 copy-start.2
  2.5 0.7 %copy-done.2 = f32[3,128,7]{1,2,0:T(8,128)S(1)} copy-done((f32[3,128,7]{1,2,0:T(8,128)S(1)}, f32[3,128,7]{1,2,0:T(8,128)}, u32[]{:S(2)}) %copy-start.2) | copy-done | bytes 10776
  3.2 22.8 %shard_map.46 = bf16[128,256]{1,0:T(8,128)(2,1)S(1)} custom-call(bf16[3,128,256]{2,1,0:T(8,128)(2,1)S(1)} %copy-done, f32[32,1024]{1,0:T(8,128)S(1)} %copy-done.1, f32[3,7,128]{2,1,0:T(8,128)S(1)} %bitcast.2, f32[1,32]{1,0:T(1,128)S(1)} %bitcast.3), custom_call_target="tpu_custom_call" | custom-call | tf_op jit(solution)/shard_map/pallas_call | solution.py:400
  26.0 0.6 %copy.6 = bf16[128,256]{1,0:T(8,128)(2,1)} copy(bf16[128,256]{1,0:T(8,128)(2,1)S(1)} %shard_map.46) | data formatting | bytes 131072
Async XLA Ops:
  0.0 0.7 %copy-start.3 = (f32[32]{0:T(128)S(1)}, f32[32]{0:T(128)}, u32[]{:S(2)}) copy-start(f32[32]{0:T(128)} %param.7) | copy-start | bytes 388
  0.7 0.9 %copy-start = (bf16[3,128,256]{2,1,0:T(8,128)(2,1)S(1)}, bf16[3,128,256]{2,1,0:T(8,128)(2,1)}, u32[]{:S(2)}) copy-start(bf16[3,128,256]{2,1,0:T(8,128)(2,1)} %streams_in.1) | copy-start | bytes 589828
  1.6 0.9 %copy-start.1 = (f32[32,1024]{1,0:T(8,128)S(1)}, f32[32,1024]{1,0:T(8,128)}, u32[]{:S(2)}) copy-start(f32[32,1024]{1,0:T(8,128)} %filt_in.1) | copy-start | bytes 393220
  2.5 0.7 %copy-start.2 = (f32[3,128,7]{1,2,0:T(8,128)S(1)}, f32[3,128,7]{1,2,0:T(8,128)}, u32[]{:S(2)}) copy-start(f32[3,128,7]{1,2,0:T(8,128)} %param.5) | copy-start | bytes 32260

commit v2 on v1

--- a/solution.py
+++ b/solution.py
@@ -150,9 +150,11 @@
     ch_count,
     streams_in,
     filt_in,
+    taps_hbm,
+    gains_hbm,
+    out,
     taps_in,
     gains_in,
-    out,
     streams,
     filt,
     send_x,
@@ -199,21 +201,12 @@
 
     load_f = pltpu.make_async_copy(filt_in, filt, load_sem.at[0])
     load_x = pltpu.make_async_copy(streams_in, streams, load_sem.at[1])
+    load_x.start()
     load_f.start()
-    load_x.start()
-    lane = lax.broadcasted_iota(jnp.int32, (tap_count, LANES), 1)
-    for c in range(GROUP):
-        for i in range(3):
-            column = jnp.sum(jnp.where(lane == GROUP * mine + c, taps_in[i], 0.0), axis=1, keepdims=True)
-            tap_rows[pl.ds(32 * i + c, tap_count, stride=GROUP), :] = jnp.broadcast_to(column, (tap_count, LANES))
-    rows[0:base, :] = jnp.zeros((base, LANES), f32)
-    for i in range(3):
-        got_x[i, :, 0:LANES] = jnp.zeros((GROUP, LANES), bf16)
-    got_f[:, 0:LANES] = jnp.zeros((GROUP, LANES), bf16)
-
-    load_f.wait()
-    for s in range(seq_count):
-        send_f[s] = filt[GROUP * s : GROUP * (s + 1), :].astype(bf16)
+    load_t = pltpu.make_async_copy(taps_hbm, taps_in, load_sem.at[2])
+    load_g = pltpu.make_async_copy(gains_hbm, gains_in, load_sem.at[3])
+    load_t.start()
+    load_g.start()
     load_x.wait()
 
     @pl.loop(0, streams.shape[1] // 16)
@@ -224,6 +217,9 @@
             for e in range(4):
                 send_x[4 * m + e, i] = values[4 * e : 4 * e + 4].astype(bf16)
 
+    load_f.wait()
+    for s in range(seq_count):
+        send_f[s] = filt[GROUP * s : GROUP * (s + 1), :].astype(bf16)
     pl.semaphore_wait(barrier, count - 1)
 
     def filter_copy(s_to, s_from):
@@ -267,6 +263,18 @@
     def _(step):
         other, s, c = peer(step)
         stream_copy(other, s, c, me).start()
+
+    load_t.wait()
+    load_g.wait()
+    lane = lax.broadcasted_iota(jnp.int32, (tap_count, LANES), 1)
+    for c in range(GROUP):
+        for i in range(3):
+            column = jnp.sum(jnp.where(lane == GROUP * mine + c, taps_in[i], 0.0), axis=1, keepdims=True)
+            tap_rows[pl.ds(32 * i + c, tap_count, stride=GROUP), :] = jnp.broadcast_to(column, (tap_count, LANES))
+    rows[0:base, :] = jnp.zeros((base, LANES), f32)
+    for i in range(3):
+        got_x[i, :, 0:LANES] = jnp.zeros((GROUP, LANES), bf16)
+    got_f[:, 0:LANES] = jnp.zeros((GROUP, LANES), bf16)
 
     got_f[:, pl.ds(pl.multiple_of(LANES + seq_pos * span_f, LANES), span_f)] = send_f[seq_pos]
     for i in range(3):
@@ -302,14 +310,21 @@
         qk = jnp.concatenate(r[:2], axis=0)
         taps.append([jnp.concatenate([t] * 4, axis=1) for t in (qk, r[2])])
 
-    @pl.loop(0, blocks // 4)
-    def _(n):
-        for e in range(2):
-            source = 2 * n + e
-
-            @pl.when(source != me)
-            def _():
-                stream_copy(source, source // ch_count, lax.rem(source, ch_count), source).wait_recv()
+    pairs = count // 2
+    start = me // 2
+
+    def arrived(source, needed):
+        @pl.when(needed & (source != me))
+        def _():
+            stream_copy(source, source // ch_count, lax.rem(source, ch_count), source).wait_recv()
+
+    arrived(2 * start + 1, True)
+
+    @pl.loop(0, pairs)
+    def _(turn):
+        n = lax.rem(start - turn + pairs, pairs)
+        arrived(2 * n, True)
+        arrived(lax.rem(2 * n - 1 + count, count), turn < pairs - 1)
 
         at = pl.ds(pl.multiple_of(n * chunk, LANES), chunk + LANES)
         q, k, v = [got_x[i, :, at].astype(f32) for i in range(3)]
@@ -395,14 +410,16 @@
     blocks = length // LANES
     dma = pltpu.SemaphoreType.DMA
     f32, bf16 = jnp.float32, jnp.bfloat16
-    anywhere = pl.BlockSpec(memory_space=pl.ANY)
+    anywhere = pl.BlockSpec(memory_space=pltpu.MemorySpace.HBM)
     inside = pl.BlockSpec(memory_space=pltpu.VMEM)
     return pl.pallas_call(
         functools.partial(owner_kernel, seq_count, ch_count),
         out_shape=jax.ShapeDtypeStruct((channels, width), bf16),
-        in_specs=[anywhere, anywhere, inside, inside],
+        in_specs=[anywhere] * 4,
         out_specs=inside,
         scratch_shapes=[
+            pltpu.VMEM((3, conv_taps.shape[2], channels), f32),
+            pltpu.VMEM((1, skip_gain.shape[0]), f32),
             pltpu.VMEM(streams.shape, bf16),
             pltpu.VMEM(long_filter.shape, f32),
             pltpu.VMEM((count, 3, GROUP, width), bf16),
@@ -416,7 +433,7 @@
             pltpu.VMEM((GROUP, blocks // 2, LANES), f32),
             pltpu.VMEM((count, 8, LANES), bf16),
             pltpu.VMEM((count, 8, LANES), bf16),
-            dma((2,)),
+            dma((4,)),
             dma((count,)),
             dma((count,)),
             dma((seq_count,)),

time: 26.9 us -> 26 us (0.967)
  Pallas kernels: 22.8 us -> 21.9 us
    pallas_call x1, Pallas kernels: 22.8 us -> 21.9 us  [owner_local(): pl.pallas_call(functools.partial(owner_kernel, seq_count, ch_count), out_...]
where the time goes in v2:
time: 26 us; the launch traced here: 25.7 us
  Pallas kernels  21.9 us (84%)
  local copies, waits for them, and re-layouts  3.82 us (15%)
    pallas_call x1, Pallas kernels, owner_local(): pl.pallas_call(functools.partial(owner_kernel, seq_count, ch_count), out_...  21.9 us
    unnamed x9, local copies, waits for them, and re-layouts  3.82 us

profile of v2, /device:TPU:0, one launch (start us, length us, event | category | flops | bytes accessed | tf_op | source)
XLA Modules:
  0.0 25.7 jit_solution(9525456026097741967)
XLA Ops:
  0.0 0.0 copy-start.3
  0.0 0.7 %copy-done.3 = f32[32]{0:T(128)S(1)} copy-done((f32[32]{0:T(128)S(1)}, f32[32]{0:T(128)}, u32[]{:S(2)}) %copy-start.3) | copy-done | bytes 152
  0.7 0.0 copy-start
  0.7 0.9 %copy-done = bf16[3,128,256]{2,1,0:T(8,128)(2,1)S(1)} copy-done((bf16[3,128,256]{2,1,0:T(8,128)(2,1)S(1)}, bf16[3,128,256]{2,1,0:T(8,128)(2,1)}, u32[]{:S(2)}) %copy-start) | copy-done | bytes 196632
  1.6 0.0 copy-start.1
  1.6 0.9 %copy-done.1 = f32[32,1024]{1,0:T(8,128)S(1)} copy-done((f32[32,1024]{1,0:T(8,128)S(1)}, f32[32,1024]{1,0:T(8,128)}, u32[]{:S(2)}) %copy-start.1) | copy-done | bytes 131096
  2.5 0.0 copy-start.2
  2.5 0.7 %copy-done.2 = f32[3,128,7]{1,2,0:T(8,128)S(1)} copy-done((f32[3,128,7]{1,2,0:T(8,128)S(1)}, f32[3,128,7]{1,2,0:T(8,128)}, u32[]{:S(2)}) %copy-start.2) | copy-done | bytes 10776
  3.2 21.9 %shard_map.46 = bf16[128,256]{1,0:T(8,128)(2,1)S(1)} custom-call(bf16[3,128,256]{2,1,0:T(8,128)(2,1)S(1)} %copy-done, f32[32,1024]{1,0:T(8,128)S(1)} %copy-done.1, f32[3,7,128]{2,1,0:T(8,128)S(1)} %bitcast.2, f32[1,32]{1,0:T(1,128)S(1)} %bitcast.3), custom_call_target="tpu_custom_call" | custom-call | tf_op jit(solution)/shard_map/pallas_call | solution.py:415
  25.1 0.6 %copy.6 = bf16[128,256]{1,0:T(8,128)(2,1)} copy(bf16[128,256]{1,0:T(8,128)(2,1)S(1)} %shard_map.46) | data formatting | bytes 131072
Async XLA Ops:
  0.0 0.7 %copy-start.3 = (f32[32]{0:T(128)S(1)}, f32[32]{0:T(128)}, u32[]{:S(2)}) copy-start(f32[32]{0:T(128)} %param.7) | copy-start | bytes 388
  0.7 0.9 %copy-start = (bf16[3,128,256]{2,1,0:T(8,128)(2,1)S(1)}, bf16[3,128,256]{2,1,0:T(8,128)(2,1)}, u32[]{:S(2)}) copy-start(bf16[3,128,256]{2,1,0:T(8,128)(2,1)} %streams_in.1) | copy-start | bytes 589828
  1.6 0.9 %copy-start.1 = (f32[32,1024]{1,0:T(8,128)S(1)}, f32[32,1024]{1,0:T(8,128)}, u32[]{:S(2)}) copy-start(f32[32,1024]{1,0:T(8,128)} %filt_in.1) | copy-start | bytes 393220
  2.5 0.7 %copy-start.2 = (f32[3,128,7]{1,2,0:T(8,128)S(1)}, f32[3,128,7]{1,2,0:T(8,128)}, u32[]{:S(2)}) copy-start(f32[3,128,7]{1,2,0:T(8,128)} %param.5) | copy-start | bytes 32260

commit v3 on v2

--- a/solution.py
+++ b/solution.py
@@ -249,8 +249,8 @@
         return pltpu.make_async_remote_copy(
             src_ref=send_o.at[other],
             dst_ref=got_o.at[source],
-            send_sem=o_send.at[other],
-            recv_sem=o_recv.at[source],
+            send_sem=o_send,
+            recv_sem=o_recv,
             device_id=(other // ch_count, lax.rem(other, ch_count)),
             device_id_type=MESH,
         )
@@ -384,10 +384,16 @@
         other, s, c = peer(step)
         stream_copy(other, s, c, me).wait_send()
 
-    @pl.loop(1, count)
-    def _(step):
-        other, s, c = peer(step)
-        out_copy(other, c * seq_count + s).wait_recv()
+    others = pl.ds(0, count - 1)
+    whole = pltpu.make_async_remote_copy(
+        src_ref=send_o.at[others],
+        dst_ref=got_o.at[others],
+        send_sem=o_send,
+        recv_sem=o_recv,
+        device_id=(seq_pos, ch_pos),
+        device_id_type=MESH,
+    )
+    whole.wait_recv()
 
     @pl.loop(0, count // 4)
     def _(m):
@@ -397,9 +403,7 @@
             piece = jnp.concatenate([p[4 * side : 4 * side + 4] for p in parts], axis=0)
             out[at, LANES * side : LANES * (side + 1)] = piece.astype(bf16)
 
-    @pl.loop(1, count)
-    def _(step):
-        out_copy(lax.rem(me + step, count), mine).wait_send()
+    whole.wait_send()
 
 
 def owner_local(streams, conv_taps, long_filter, skip_gain):
@@ -438,8 +442,8 @@
             dma((count,)),
             dma((seq_count,)),
             dma((seq_count,)),
-            dma((count,)),
-            dma((count,)),
+            dma(()),
+            dma(()),
         ],
         compiler_params=pltpu.CompilerParams(
             collective_id=0, has_side_effects=True, vmem_limit_bytes=48 * 1024 * 1024

time: 26 us -> 25.1 us (0.965)
  Pallas kernels: 21.9 us -> 21 us
    pallas_call x1, Pallas kernels: 21.9 us -> 21 us  [owner_local(): pl.pallas_call(functools.partial(owner_kernel, seq_count, ch_count), out_...]
where the time goes in v3:
time: 25.1 us; the launch traced here: 24.9 us
  Pallas kernels  21 us (84%)
  local copies, waits for them, and re-layouts  3.82 us (15%)
    pallas_call x1, Pallas kernels, owner_local(): pl.pallas_call(functools.partial(owner_kernel, seq_count, ch_count), out_...  21 us
    unnamed x9, local copies, waits for them, and re-layouts  3.82 us

profile of v3, /device:TPU:0, one launch (start us, length us, event | category | flops | bytes accessed | tf_op | source)
XLA Modules:
  0.0 24.9 jit_solution(6658741300385905399)
XLA Ops:
  0.0 0.0 copy-start.3
  0.0 0.7 %copy-done.3 = f32[32]{0:T(128)S(1)} copy-done((f32[32]{0:T(128)S(1)}, f32[32]{0:T(128)}, u32[]{:S(2)}) %copy-start.3) | copy-done | bytes 152
  0.7 0.0 copy-start
  0.7 0.9 %copy-done = bf16[3,128,256]{2,1,0:T(8,128)(2,1)S(1)} copy-done((bf16[3,128,256]{2,1,0:T(8,128)(2,1)S(1)}, bf16[3,128,256]{2,1,0:T(8,128)(2,1)}, u32[]{:S(2)}) %copy-start) | copy-done | bytes 196632
  1.6 0.0 copy-start.1
  1.6 0.9 %copy-done.1 = f32[32,1024]{1,0:T(8,128)S(1)} copy-done((f32[32,1024]{1,0:T(8,128)S(1)}, f32[32,1024]{1,0:T(8,128)}, u32[]{:S(2)}) %copy-start.1) | copy-done | bytes 131096
  2.5 0.0 copy-start.2
  2.5 0.7 %copy-done.2 = f32[3,128,7]{1,2,0:T(8,128)S(1)} copy-done((f32[3,128,7]{1,2,0:T(8,128)S(1)}, f32[3,128,7]{1,2,0:T(8,128)}, u32[]{:S(2)}) %copy-start.2) | copy-done | bytes 10776
  3.2 21.0 %shard_map.46 = bf16[128,256]{1,0:T(8,128)(2,1)S(1)} custom-call(bf16[3,128,256]{2,1,0:T(8,128)(2,1)S(1)} %copy-done, f32[32,1024]{1,0:T(8,128)S(1)} %copy-done.1, f32[3,7,128]{2,1,0:T(8,128)S(1)} %bitcast.2, f32[1,32]{1,0:T(1,128)S(1)} %bitcast.3), custom_call_target="tpu_custom_call" | custom-call | tf_op jit(solution)/shard_map/pallas_call | solution.py:419
  24.2 0.6 %copy.6 = bf16[128,256]{1,0:T(8,128)(2,1)} copy(bf16[128,256]{1,0:T(8,128)(2,1)S(1)} %shard_map.46) | data formatting | bytes 131072
Async XLA Ops:
  0.0 0.7 %copy-start.3 = (f32[32]{0:T(128)S(1)}, f32[32]{0:T(128)}, u32[]{:S(2)}) copy-start(f32[32]{0:T(128)} %param.7) | copy-start | bytes 388
  0.7 0.9 %copy-start = (bf16[3,128,256]{2,1,0:T(8,128)(2,1)S(1)}, bf16[3,128,256]{2,1,0:T(8,128)(2,1)}, u32[]{:S(2)}) copy-start(bf16[3,128,256]{2,1,0:T(8,128)(2,1)} %streams_in.1) | copy-start | bytes 589828
  1.6 0.9 %copy-start.1 = (f32[32,1024]{1,0:T(8,128)S(1)}, f32[32,1024]{1,0:T(8,128)}, u32[]{:S(2)}) copy-start(f32[32,1024]{1,0:T(8,128)} %filt_in.1) | copy-start | bytes 393220
  2.5 0.7 %copy-start.2 = (f32[3,128,7]{1,2,0:T(8,128)S(1)}, f32[3,128,7]{1,2,0:T(8,128)}, u32[]{:S(2)}) copy-start(f32[3,128,7]{1,2,0:T(8,128)} %param.5) | copy-start | bytes 32260

commit v4 on v3

--- a/solution.py
+++ b/solution.py
@@ -227,8 +227,8 @@
         return pltpu.make_async_remote_copy(
             src_ref=send_f.at[s_to],
             dst_ref=got_f.at[:, at],
-            send_sem=f_send.at[s_to],
-            recv_sem=f_recv.at[s_from],
+            send_sem=f_send,
+            recv_sem=f_recv,
             device_id=(s_to, ch_pos),
             device_id_type=MESH,
         )
@@ -239,7 +239,7 @@
         return pltpu.make_async_remote_copy(
             src_ref=send_x.at[block],
             dst_ref=got_x.at[:, :, at],
-            send_sem=x_send.at[other],
+            send_sem=x_send,
             recv_sem=x_recv.at[source],
             device_id=(s, c),
             device_id_type=MESH,
@@ -280,10 +280,16 @@
     for i in range(3):
         got_x[i, :, pl.ds(pl.multiple_of(LANES + me * width, LANES), width)] = send_x[mine, i]
 
-    @pl.loop(1, seq_count)
-    def _(step):
-        source = lax.rem(seq_pos + step, seq_count)
-        filter_copy(source, source).wait_recv()
+    slots = pl.ds(0, seq_count - 1)
+    filters = pltpu.make_async_remote_copy(
+        src_ref=send_f.at[slots],
+        dst_ref=send_f.at[slots],
+        send_sem=f_send,
+        recv_sem=f_recv,
+        device_id=(seq_pos, ch_pos),
+        device_id_type=MESH,
+    )
+    filters.wait_recv()
 
     row_at = lax.broadcasted_iota(jnp.int32, (LANES, LANES), 0)
     lane_at = lax.broadcasted_iota(jnp.int32, (LANES, LANES), 1)
@@ -375,16 +381,16 @@
 
     got_o[mine] = send_o[me]
 
-    @pl.loop(1, seq_count)
-    def _(step):
-        filter_copy(lax.rem(seq_pos + step, seq_count), seq_pos).wait_send()
-
-    @pl.loop(1, count)
-    def _(step):
-        other, s, c = peer(step)
-        stream_copy(other, s, c, me).wait_send()
-
     others = pl.ds(0, count - 1)
+    filters.wait_send()
+    pltpu.make_async_remote_copy(
+        src_ref=send_x.at[others],
+        dst_ref=send_x.at[others],
+        send_sem=x_send,
+        recv_sem=x_recv.at[me],
+        device_id=(seq_pos, ch_pos),
+        device_id_type=MESH,
+    ).wait_send()
     whole = pltpu.make_async_remote_copy(
         src_ref=send_o.at[others],
         dst_ref=got_o.at[others],
@@ -438,10 +444,10 @@
             pltpu.VMEM((count, 8, LANES), bf16),
             pltpu.VMEM((count, 8, LANES), bf16),
             dma((4,)),
+            dma(()),
             dma((count,)),
-            dma((count,)),
-            dma((seq_count,)),
-            dma((seq_count,)),
+            dma(()),
+            dma(()),
             dma(()),
             dma(()),
         ],

time: 25.1 us -> 24.7 us (0.984)
  Pallas kernels: 21 us -> 20.6 us
    pallas_call x1, Pallas kernels: 21 us -> 20.6 us  [owner_local(): pl.pallas_call(functools.partial(owner_kernel, seq_count, ch_count), out_...]
where the time goes in v4:
time: 24.7 us; the launch traced here: 24.5 us
  Pallas kernels  20.6 us (83%)
  local copies, waits for them, and re-layouts  3.82 us (15%)
    pallas_call x1, Pallas kernels, owner_local(): pl.pallas_call(functools.partial(owner_kernel, seq_count, ch_count), out_...  20.6 us
    unnamed x9, local copies, waits for them, and re-layouts  3.82 us

profile of v4, /device:TPU:0, one launch (start us, length us, event | category | flops | bytes accessed | tf_op | source)
XLA Modules:
  0.0 24.5 jit_solution(2056603281580150230)
XLA Ops:
  0.0 0.0 copy-start.3
  0.0 0.7 %copy-done.3 = f32[32]{0:T(128)S(1)} copy-done((f32[32]{0:T(128)S(1)}, f32[32]{0:T(128)}, u32[]{:S(2)}) %copy-start.3) | copy-done | bytes 152
  0.7 0.0 copy-start
  0.7 0.9 %copy-done = bf16[3,128,256]{2,1,0:T(8,128)(2,1)S(1)} copy-done((bf16[3,128,256]{2,1,0:T(8,128)(2,1)S(1)}, bf16[3,128,256]{2,1,0:T(8,128)(2,1)}, u32[]{:S(2)}) %copy-start) | copy-done | bytes 196632
  1.6 0.0 copy-start.1
  1.6 0.9 %copy-done.1 = f32[32,1024]{1,0:T(8,128)S(1)} copy-done((f32[32,1024]{1,0:T(8,128)S(1)}, f32[32,1024]{1,0:T(8,128)}, u32[]{:S(2)}) %copy-start.1) | copy-done | bytes 131096
  2.5 0.0 copy-start.2
  2.5 0.7 %copy-done.2 = f32[3,128,7]{1,2,0:T(8,128)S(1)} copy-done((f32[3,128,7]{1,2,0:T(8,128)S(1)}, f32[3,128,7]{1,2,0:T(8,128)}, u32[]{:S(2)}) %copy-start.2) | copy-done | bytes 10776
  3.2 20.6 %shard_map.46 = bf16[128,256]{1,0:T(8,128)(2,1)S(1)} custom-call(bf16[3,128,256]{2,1,0:T(8,128)(2,1)S(1)} %copy-done, f32[32,1024]{1,0:T(8,128)S(1)} %copy-done.1, f32[3,7,128]{2,1,0:T(8,128)S(1)} %bitcast.2, f32[1,32]{1,0:T(1,128)S(1)} %bitcast.3), custom_call_target="tpu_custom_call" | custom-call | tf_op jit(solution)/shard_map/pallas_call | solution.py:425
  23.8 0.6 %copy.6 = bf16[128,256]{1,0:T(8,128)(2,1)} copy(bf16[128,256]{1,0:T(8,128)(2,1)S(1)} %shard_map.46) | data formatting | bytes 131072
Async XLA Ops:
  0.0 0.7 %copy-start.3 = (f32[32]{0:T(128)S(1)}, f32[32]{0:T(128)}, u32[]{:S(2)}) copy-start(f32[32]{0:T(128)} %param.7) | copy-start | bytes 388
  0.7 0.9 %copy-start = (bf16[3,128,256]{2,1,0:T(8,128)(2,1)S(1)}, bf16[3,128,256]{2,1,0:T(8,128)(2,1)}, u32[]{:S(2)}) copy-start(bf16[3,128,256]{2,1,0:T(8,128)(2,1)} %streams_in.1) | copy-start | bytes 589828
  1.6 0.9 %copy-start.1 = (f32[32,1024]{1,0:T(8,128)S(1)}, f32[32,1024]{1,0:T(8,128)}, u32[]{:S(2)}) copy-start(f32[32,1024]{1,0:T(8,128)} %filt_in.1) | copy-start | bytes 393220
  2.5 0.7 %copy-start.2 = (f32[3,128,7]{1,2,0:T(8,128)S(1)}, f32[3,128,7]{1,2,0:T(8,128)}, u32[]{:S(2)}) copy-start(f32[3,128,7]{1,2,0:T(8,128)} %param.5) | copy-start | bytes 32260
